TPU v7x, 32 devices: a whole 2x2x4 slice. The times are simulated.
32 devices in a mesh: grp: 4 (over z), seq: 8 (over y, x, core).
Axes of the slice: x: 2, y: 2, z: 4, core: 2. Of those that a mesh axis runs over, the one named last changes fastest.
Arguments:
- tokens: bfloat16 [4096, 2048], P(('grp', 'seq')), may hold values from -6 to 6
- norm_gains: float32 [2, 2048], replicated, may hold values from 0.5 to 1.5
- norm_biases: float32 [2, 2048], replicated, may hold values from -1 to 1
- mix_weight: bfloat16 [2048, 3, 2048], P(None, None, 'seq'), may hold values from -0.125 to 0.125
- mix_bias: bfloat16 [3, 2048], P(None, 'seq'), may hold values from -1.796875 to 1.796875
- out_weight: bfloat16 [2048, 2048], P('seq'), may hold values from -0.5 to 0.5
- gate_up_weight: bfloat16 [2048, 2, 5632], P(None, None, 'seq'), may hold values from -0.125 to 0.125
- down_weight: bfloat16 [5632, 2048], P('seq'), may hold values from -0.078125 to 0.078125
- row_lengths: int32 [8], replicated, may hold values from 128 to 1024, as said below
- row_group: int32 [8], replicated, may hold values from 0 to 3, as said below
- cotangent: bfloat16 [4096, 2048], P(('grp', 'seq')), may hold values from -6 to 6
Outputs:
- layer_out: bfloat16 [4096, 2048], P(('grp', 'seq'))
- tokens_grad: bfloat16 [4096, 2048], P(('grp', 'seq'))
- gains_grad: float32 [2, 2048], replicated
- biases_grad: float32 [2, 2048], replicated
- mix_grad: float32 [2048, 3, 2048], P(None, None, 'seq')
- mix_bias_grad: float32 [3, 2048], P(None, 'seq')
- out_grad: float32 [2048, 2048], P('seq')
- gate_up_grad: float32 [2048, 2, 5632], P(None, None, 'seq')
- down_grad: float32 [5632, 2048], P('seq')
Inputs may be any that keep to these rules, and one draw needn't show every extreme that they name: `row_lengths`: rows 0 to 1 are 1024 long; every other row's length is a multiple of 128 and at most 256. `row_group`: each of rows 0 to 1 fills a group alone; every other group holds exactly three of the other rows.
All inputs are finite; a program needn't handle non-finite values.
Results may differ from a plain program's by a relative error of at most 0.02.
Values may be sent and summed in bfloat16 or wider, within the bound.
A program may use at most 320 MiB of HBM per device.

v0:
```python
import math
import jax
import jax.numpy as jnp
from jax import lax
from jax.sharding import PartitionSpec as P

HEAD_DIM = 64
ROT = 16
EPS = 1e-05
NEG = -1e30
BASE = 10000.0


def layer_norm(values, gain, bias):
    centered = values - jnp.mean(values, axis=-1, keepdims=True)
    scale = lax.rsqrt(jnp.mean(centered * centered, axis=-1, keepdims=True) + EPS)
    unit = centered * scale
    return (unit * gain + bias, unit, scale)


def norm_back(incoming, unit, scale, gain):
    along = incoming * gain
    inner = jnp.mean(along, axis=-1, keepdims=True)
    cross = jnp.mean(along * unit, axis=-1, keepdims=True)
    return (
        scale * (along - inner - unit * cross),
        jnp.sum(incoming * unit, axis=0),
        jnp.sum(incoming, axis=0),
    )


def rotate(values, where, sign):
    half = ROT // 2
    freq = BASE ** (-jnp.arange(half, dtype=jnp.float32) / half)
    angle = where.astype(jnp.float32)[:, None] * freq[None, :]
    cosine = jnp.cos(angle)[:, None, :]
    sine = sign * jnp.sin(angle)[:, None, :]
    first = values[..., :half]
    second = values[..., half:ROT]
    return jnp.concatenate(
        [first * cosine - second * sine, second * cosine + first * sine, values[..., ROT:]], axis=-1
    )


def unrotate(lowered, where):
    wide = lowered.astype(jnp.float32)
    turned = jnp.stack(
        [rotate(wide[:, 0], where, -1.0), rotate(wide[:, 1], where, -1.0), wide[:, 2]], axis=1
    )
    return turned.reshape(lowered.shape[0], 3, -1).astype(jnp.bfloat16)


def slot_rows(row_lengths, row_group, group, slots):
    order = jnp.arange(row_lengths.shape[0], dtype=jnp.int32)
    same = row_group == group
    earlier = (order[:, None] > order[None, :]) & same[None, :]
    begin = jnp.sum(jnp.where(earlier, row_lengths[None, :], 0), axis=1)
    finish = begin + row_lengths
    inside = same[None, :] & (slots[:, None] >= begin[None, :]) & (slots[:, None] < finish[None, :])
    label = jnp.sum(jnp.where(inside, order[None, :] + 1, 0), axis=1) - 1
    offset = jnp.sum(jnp.where(inside, slots[:, None] - begin[None, :], 0), axis=1)
    load = jnp.sum(jnp.where(same, row_lengths, 0))
    return (label, jnp.where(label < 0, slots - load, offset))


def block_scores(query, key, label, start, block):
    part = lax.dynamic_slice_in_dim(query, start, block, 0)
    rows = start + jnp.arange(block, dtype=jnp.int32)
    columns = jnp.arange(label.shape[0], dtype=jnp.int32)
    label_rows = lax.dynamic_slice_in_dim(label, start, block, 0)
    allowed = (label_rows[:, None] == label[None, :]) & (rows[:, None] >= columns[None, :])
    scores = jnp.einsum("qhe,khe->hqk", part, key, preferred_element_type=jnp.float32) * (
        1.0 / math.sqrt(query.shape[-1])
    )
    return (part, jnp.where(allowed[None], scores, NEG))


def attend(query, key, value, label, block):

    def one_block(index):
        part, scores = block_scores(query, key, label, index * block, block)
        top = jnp.max(scores, axis=-1, keepdims=True)
        weights = jnp.exp(scores - top)
        totals = jnp.sum(weights, axis=-1, keepdims=True)
        probs = (weights / totals).astype(jnp.bfloat16)
        mixed = jnp.einsum("hqk,khe->qhe", probs, value, preferred_element_type=jnp.float32)
        return (mixed, top[..., 0] + jnp.log(totals[..., 0]))

    mixed, log_totals = lax.map(one_block, jnp.arange(query.shape[0] // block, dtype=jnp.int32))
    return (mixed.reshape(query.shape), log_totals)


def attend_back(query, key, value, label, log_totals, mixed_back, block):
    scale = 1.0 / math.sqrt(query.shape[-1])

    def one_block(carry, index):
        key_back, value_back = carry
        start = index * block
        part, scores = block_scores(query, key, label, start, block)
        back_part = lax.dynamic_slice_in_dim(mixed_back, start, block, 0)
        probs = jnp.exp(scores - log_totals[index][..., None])
        value_back = value_back + jnp.einsum(
            "hqk,qhe->khe",
            probs.astype(jnp.bfloat16),
            back_part,
            preferred_element_type=jnp.float32,
        )
        probs_back = jnp.einsum(
            "qhe,khe->hqk", back_part, value, preferred_element_type=jnp.float32
        )
        inner = jnp.sum(probs_back * probs, axis=-1, keepdims=True)
        score_back = (probs * (probs_back - inner)).astype(jnp.bfloat16)
        query_back = (
            jnp.einsum("hqk,khe->qhe", score_back, key, preferred_element_type=jnp.float32) * scale
        )
        key_back = (
            key_back
            + jnp.einsum("hqk,qhe->khe", score_back, part, preferred_element_type=jnp.float32)
            * scale
        )
        return ((key_back, value_back), query_back)

    empty = jnp.zeros(key.shape, jnp.float32)
    (key_back, value_back), query_back = lax.scan(
        one_block, (empty, empty), jnp.arange(query.shape[0] // block, dtype=jnp.int32)
    )
    return (query_back.reshape(query.shape), key_back, value_back)


def silu_parts(gate_up):
    gate = gate_up[:, 0]
    upper = gate_up[:, 1]
    sigma = jax.nn.sigmoid(gate)
    return (gate * sigma * upper, gate, upper, sigma)


def gate_back(hidden_back, gate, upper, sigma):
    gate_part = hidden_back * upper * sigma * (1.0 + gate * (1.0 - sigma))
    up_part = hidden_back * gate * sigma
    return jnp.stack([gate_part, up_part], axis=1).astype(jnp.bfloat16)


def gather_rows(values):
    return lax.all_gather(values, "seq", axis=0, tiled=True)


def summed_rows(product, left):
    return lax.psum_scatter(
        product(left).astype(jnp.bfloat16), "seq", scatter_dimension=0, tiled=True
    ).astype(jnp.float32)


def on_device(
    tokens,
    norm_gains,
    norm_biases,
    mix_weight,
    mix_bias,
    out_weight,
    gate_up_weight,
    down_weight,
    row_lengths,
    row_group,
    cotangent,
):
    seq_count = lax.axis_size("seq")
    shard = lax.axis_index("seq")
    group = lax.axis_index("grp")
    slots_dev = tokens.shape[0]
    width = tokens.shape[1]
    group_slots = slots_dev * seq_count
    block = min(512, group_slots)
    local_width = width // seq_count
    local_heads = local_width // HEAD_DIM
    mine = shard * slots_dev + jnp.arange(slots_dev, dtype=jnp.int32)
    label_mine, place_mine = slot_rows(row_lengths, row_group, group, mine)
    label_all, place_all = slot_rows(
        row_lengths, row_group, group, jnp.arange(group_slots, dtype=jnp.int32)
    )
    inputs = tokens.astype(jnp.float32)
    upstream = cotangent.astype(jnp.float32) * (label_mine >= 0).astype(jnp.float32)[:, None]
    upstream_low = upstream.astype(jnp.bfloat16)
    normed, unit_one, scale_one = layer_norm(inputs, norm_gains[0], norm_biases[0])
    normed_low = normed.astype(jnp.bfloat16)
    mix_full, bias_full, out_full = (
        lax.all_gather(mix_weight, "seq", axis=2, tiled=True),
        lax.all_gather(mix_bias, "seq", axis=1, tiled=True),
        lax.all_gather(out_weight, "seq", axis=0, tiled=True),
    )
    mixin = jnp.einsum(
        "td,dcf->tcf", normed_low, mix_full, preferred_element_type=jnp.float32
    ) + bias_full.astype(jnp.float32)
    heads_in = mixin.reshape(slots_dev, 3, width // HEAD_DIM, HEAD_DIM)
    sending = jnp.stack(
        [
            rotate(heads_in[:, 0], place_mine, 1.0),
            rotate(heads_in[:, 1], place_mine, 1.0),
            heads_in[:, 2],
        ],
        axis=1,
    ).astype(jnp.bfloat16)
    arrived = lax.all_to_all(
        sending.reshape(slots_dev, 3, seq_count, local_width),
        "seq",
        split_axis=2,
        concat_axis=0,
        tiled=True,
    )
    arrived = arrived.reshape(group_slots, 3, local_heads, HEAD_DIM)
    query, key, value = (arrived[:, 0], arrived[:, 1], arrived[:, 2])
    mixed, log_totals = attend(query, key, value, label_all, block)
    attended = lax.all_to_all(
        mixed.reshape(group_slots, local_width).astype(jnp.bfloat16),
        "seq",
        split_axis=0,
        concat_axis=1,
        tiled=True,
    )
    resid = inputs + jnp.dot(attended, out_full, preferred_element_type=jnp.float32)
    normed_two, unit_two, scale_two = layer_norm(resid, norm_gains[1], norm_biases[1])
    normed_two_all = gather_rows(normed_two.astype(jnp.bfloat16))
    gate_up = jnp.einsum(
        "td,dcf->tcf", normed_two_all, gate_up_weight, preferred_element_type=jnp.float32
    )
    hidden, gate, upper, sigma = silu_parts(gate_up)
    hidden_low = hidden.astype(jnp.bfloat16)

    def down_product(part):
        return jnp.dot(part, down_weight, preferred_element_type=jnp.float32)

    layer_out = resid + summed_rows(down_product, hidden_low)
    upstream_all = gather_rows(upstream_low)
    down_shard = jnp.einsum(
        "tf,td->fd", hidden_low, upstream_all, preferred_element_type=jnp.float32
    )
    hidden_back = jnp.einsum(
        "td,fd->tf", upstream_all, down_weight, preferred_element_type=jnp.float32
    )
    gate_up_back = gate_back(hidden_back, gate, upper, sigma)
    gate_up_shard = jnp.einsum(
        "td,tcf->dcf", normed_two_all, gate_up_back, preferred_element_type=jnp.float32
    )

    def gate_up_product(part):
        return jnp.einsum("tcf,dcf->td", part, gate_up_weight, preferred_element_type=jnp.float32)

    normed_two_back = summed_rows(gate_up_product, gate_up_back)
    resid_part, gain_two, bias_two = norm_back(normed_two_back, unit_two, scale_two, norm_gains[1])
    resid_back = upstream + resid_part
    branch_low = resid_back.astype(jnp.bfloat16)
    out_term = jnp.einsum("te,td->ed", attended, branch_low, preferred_element_type=jnp.float32)
    attended_back = jnp.einsum(
        "td,ed->te", branch_low, out_full, preferred_element_type=jnp.float32
    ).astype(jnp.bfloat16)
    heads_back = lax.all_to_all(
        attended_back, "seq", split_axis=1, concat_axis=0, tiled=True
    ).reshape(group_slots, local_heads, HEAD_DIM)
    query_back, key_back, value_back = attend_back(
        query, key, value, label_all, log_totals, heads_back, block
    )
    lowered = (
        jnp.stack([query_back, key_back, value_back], axis=1)
        .astype(jnp.bfloat16)
        .reshape(group_slots, 3, 1, local_width)
    )
    returned = lax.all_to_all(lowered, "seq", split_axis=0, concat_axis=2, tiled=True).reshape(
        slots_dev, 3, width // HEAD_DIM, HEAD_DIM
    )
    mixin_back = unrotate(returned, place_mine)
    mix_term = jnp.einsum("td,tcf->dcf", normed_low, mixin_back, preferred_element_type=jnp.float32)
    bias_term = jnp.sum(mixin_back, axis=0, dtype=jnp.float32)
    normed_back = jnp.einsum(
        "tcf,dcf->td", mixin_back, mix_full, preferred_element_type=jnp.float32
    )
    mix_shard, bias_shard, out_shard = (
        lax.psum_scatter(
            mix_term.astype(jnp.bfloat16), "seq", scatter_dimension=2, tiled=True
        ).astype(jnp.float32),
        lax.psum_scatter(
            bias_term.astype(jnp.bfloat16), "seq", scatter_dimension=1, tiled=True
        ).astype(jnp.float32),
        lax.psum_scatter(
            out_term.astype(jnp.bfloat16), "seq", scatter_dimension=0, tiled=True
        ).astype(jnp.float32),
    )
    tokens_part, gain_one, bias_one = norm_back(normed_back, unit_one, scale_one, norm_gains[0])
    tokens_grad = (resid_back + tokens_part).astype(jnp.bfloat16)
    mix_grad, mix_bias_grad, out_grad, gate_up_grad, down_grad = (
        lax.psum(mix_shard.astype(jnp.bfloat16), "grp").astype(jnp.float32),
        lax.psum(bias_shard.astype(jnp.bfloat16), "grp").astype(jnp.float32),
        lax.psum(out_shard.astype(jnp.bfloat16), "grp").astype(jnp.float32),
        lax.psum(gate_up_shard.astype(jnp.bfloat16), "grp").astype(jnp.float32),
        lax.psum(down_shard.astype(jnp.bfloat16), "grp").astype(jnp.float32),
    )
    gains_grad, biases_grad = lax.psum(
        (jnp.stack([gain_one, gain_two]), jnp.stack([bias_one, bias_two])), ("grp", "seq")
    )
    return (
        layer_out.astype(jnp.bfloat16),
        tokens_grad,
        gains_grad,
        biases_grad,
        mix_grad,
        mix_bias_grad,
        out_grad,
        gate_up_grad,
        down_grad,
    )


def solution(mesh):
    placed = (
        P(("grp", "seq"), None),
        P(),
        P(),
        P(None, None, "seq"),
        P(None, "seq"),
        P("seq", None),
        P(None, None, "seq"),
        P("seq", None),
        P(),
        P(),
        P(("grp", "seq"), None),
    )
    return jax.shard_map(
        on_device,
        mesh=mesh,
        in_specs=placed,
        out_specs=(
            P(("grp", "seq"), None),
            P(("grp", "seq"), None),
            P(),
            P(),
            P(None, None, "seq"),
            P(None, "seq"),
            P("seq", None),
            P(None, None, "seq"),
            P("seq", None),
        ),
        check_vma=False,
    )
```

profile of v0, /device:TPU:0, one launch (start us, length us, event | category | flops | bytes accessed | tf_op | source)
XLA Modules:
  0.0 1248.3 jit_solution(738130817734868844)
XLA Ops:
  9.5 10.4 all_gather.16
  21.9 121.0 %all-gather.5.cloned.1.call-done = bf16[2048,3,2048]{2,0,1:T(8,128)(2,1)} async-done(((bf16[2048,3,256]{2,0,1:T(8,128)(2,1)}), bf16[2048,3,2048]{2,0,1:T(8,128)(2,1)}) %all-gather.5.cloned.1.call-update) | async-done | bytes 25165840 | tf_op jit(solution)/shard_map/all_gather | solution.py:186
  143.0 13.4 %convolution_add_fusion = f32[128,3,2048]{2,0,1:T(8,128)} fusion(bf16[2048,3,2048]{2,0,1:T(8,128)(2,1)} %all-gather.5.cloned.1.call-done, f32[3,2048]{1,0:T(4,128)S(1)} %convert_element_type.139, bf16[128,2048]{1,0:T(8,128)(2,1)S(1)} %copy-done.5, f32[2048]{0:T(1024)S(1)} %bitcast.195, f32[2048]{0:T(1024)S(1)} %bitcast.191, f32[128]{0:T(128)S(1)} %add_rsqrt_fusion.1, ...), kind=kOutput, calls=%fused_computation.63 | convolution fusion | flops 3223584768 | bytes 28877824 | tf_op jit(solution)/shard_map/td,dcf->tcf/dot_general | solution.py:190
  156.4 3.5 copy.90
  164.7 4.5 all-to-all-start
  169.3 35.6 %all-to-all-done = bf16[128,3,8,256]{0,3,1,2:T(8,128)(2,1)} async-done(((bf16[128,3,8,256]{0,3,1,2:T(8,128)(2,1)}), bf16[128,3,8,256]{0,3,1,2:T(8,128)(2,1)}, u32[]{:S(2)}, u32[]{:S(2)}) %all-to-all-start) | async-done | bytes 1572896 | tf_op jit(solution)/shard_map/all_to_all | solution.py:202
  204.9 3.6 copy.92
  208.5 3.7 reshape.381
  212.2 2.6 slice_bitcast_fusion.6
  215.6 21.5 %while.27 = (s32[]{:T(128)}, bf16[2,512,4,64]{1,3,2,0:T(8,128)(2,1)}, f32[2,4,512]{2,1,0:T(4,128)S(1)}, s32[2]{0:T(128)S(1)}, s32[1024]{0:T(1024)S(1)}, /*index=...) while((s32[]{:T(128)}, ...), condition=%wide.region_10.11_spmd, body=%wide.region_7.10_spmd.sunk | while | flops 563608064 | bytes 35469596 | solution.py:89
  217.5 2.6 fusion.126
  222.5 3.0 fusion.128
  228.2 2.6 fusion.126
  233.3 3.0 fusion.128
  243.5 4.2 all-to-all-start.1
  247.8 9.7 all-to-all-done.1
  257.4 4.9 fusion.81
  266.9 33.4 %all-gather.9.cloned.1.call-done = bf16[1024,2048]{1,0:T(8,128)(2,1)} async-done(((bf16[128,2048]{1,0:T(8,128)(2,1)}), bf16[1024,2048]{1,0:T(8,128)(2,1)}) %all-gather.9.cloned.1.call-update) | async-done | bytes 4194320 | tf_op jit(solution)/shard_map/all_gather | solution.py:144
  300.4 11.0 fusion.39
  311.4 28.1 %all-gather.11.cloned.1.call-done = bf16[1024,2048]{1,0:T(8,128)(2,1)} async-done(((bf16[128,2048]{1,0:T(8,128)(2,1)}), bf16[1024,2048]{1,0:T(8,128)(2,1)}) %all-gather.11.cloned.1.call-update) | async-done | bytes 4194320 | tf_op jit(solution)/shard_map/all_gather | solution.py:144
  339.5 8.3 fusion.45
  349.4 11.0 bitcast_convert_fusion
  360.4 6.4 convolution_convert_fusion.3
  366.9 45.0 %reduce-scatter.10.cloned.1.call-done = bf16[128,2048]{1,0:T(8,128)(2,1)} async-done(((bf16[1024,2048]{1,0:T(8,128)(2,1)}), bf16[128,2048]{1,0:T(8,128)(2,1)}) %reduce-scatter.10.cloned.1.call-update) | async-done | bytes 524304 | tf_op jit(solution)/shard_map/reduce_scatter | solution.py:148
  414.0 53.4 %reduce-scatter.8.cloned.1.call-done = bf16[128,2048]{1,0:T(8,128)(2,1)} async-done(((bf16[1024,2048]{1,0:T(8,128)(2,1)}), bf16[128,2048]{1,0:T(8,128)(2,1)}) %reduce-scatter.8.cloned.1.call-update) | async-done | bytes 524304 | tf_op jit(solution)/shard_map/reduce_scatter | solution.py:148
  469.7 7.1 convolution_convert_fusion.1
  476.8 6.3 convolution_convert_fusion.5
  484.0 3.5 all-to-all-start.2
  487.7 9.4 all-to-all-done.2
  501.1 31.6 %while.28 = (s32[]{:T(128)}, f32[1024,4,64]{0,2,1:T(8,128)S(1)}, f32[1024,4,64]{0,2,1:T(8,128)}, bf16[2,512,4,64]{1,3,2,0:T(8,128)(2,1)}, s32[2]{0:T(128)S(1)}, ...) while((s32[]{:T(128)}, f32[1024,4,64]{0,2,1:T(8,128)S(1)}, ...), condition=%wide.region_19.20_spmd.clone, body=%wide.region_17.19_spmd.clone.sunk | while | flops 1376647680 | bytes 87103920 | solution.py:124
  506.4 2.5 fusion.141
  508.9 3.2 multiply_reduce_fusion.4
  522.2 2.6 fusion.141
  524.7 3.2 multiply_reduce_fusion.4
  537.6 3.0 copy.98
  540.5 29.5 %all_to_all.56 = bf16[1024,3,1,256]{3,1,2,0:T(4,128)(2,1)S(1)} all-to-all(bf16[1024,3,1,256]{3,1,2,0:T(4,128)(2,1)S(1)} %copy.98), channel_id=1, replica_groups=mesh['grp'=4,'seq'=8] {'seq'}, dimensions={0} | all-to-all | bytes 3145728 | tf_op jit(solution)/shard_map/all_to_all | solution.py:266
  578.5 12.0 convolution_convert_fusion
  590.6 10.8 convolution_convert_fusion.2
  603.1 8.9 convolution_convert_fusion.4
  612.0 134.7 %reduce-scatter.12.cloned.1.call-done = bf16[2048,3,256]{2,0,1:T(8,128)(2,1)} async-done(((bf16[2048,3,2048]{2,0,1:T(8,128)(2,1)}), bf16[2048,3,256]{2,0,1:T(8,128)(2,1)}) %reduce-scatter.12.cloned.1.call-update) | async-done | bytes 3145744 | tf_op jit(solution)/shard_map/reduce_scatter | solution.py:276
  746.7 14.6 %fusion.59 = (f32[2048]{0:T(1024)S(1)}, f32[128]{0:T(128)S(1)}, f32[128]{0:T(128)S(1)}, f32[2048]{0:T(1024)S(1)}, f32[128,2048]{1,0:T(8,128)}) fusion(bf16[128,2048]{1,0:T(8,128)(2,1)S(1)} %copy-done.6, f32[128]{0:T(128)S(1)} %copy-done.35, f32[128]{0:T(128)S(1)} %copy-done.33, f32[2048]{0:T(1024)S(1)} %bitcast.193, ...), kind=kOutput, calls=%fused_computation.93 | convolution fusion | flops 3225415680 | bytes 28338176 | tf_op jit(solution)/shard_map/tcf,dcf->td/dot_general | solution.py:272
  761.4 40.2 %all-reduce = (f32[2,2048]{1,0:T(2,128)}, f32[2,2048]{1,0:T(2,128)}) all-reduce(f32[2,2048]{1,0:T(2,128)S(1)} %pad_maximum_fusion.10, f32[2,2048]{1,0:T(2,128)S(1)} %pad_maximum_fusion.11), channel_id=1, replica_groups=mesh['grp'=4,'seq'=8] {'grp','seq'}, use_global_device_ids=true, to_apply=%region_24.25 | all-reduce | flops 8192 | bytes 65536 | tf_op jit(solution)/shard_map/psum | solution.py:295
  805.0 12.3 psum.52
  817.9 407.1 %all-reduce.4.cloned.1.call-done = (bf16[2048,3,256]{2,0,1:T(8,128)(2,1)}, bf16[256,2048]{1,0:T(8,128)(2,1)}, bf16[2048,2,704]{0,2,1:T(8,128)(2,1)}, bf16[704,2048]{1,0:T(8,128)(2,1)}) async-done(((bf16[2048,3,256]{2,0,1:T(8,128)(2,1)}, bf16[256,2048]{1,0:T(8,128)(2,1)}, bf16[2048,2,704]{0,2,1:T(8,128)(2,1)}, bf16[704,2048]{1,0:T(8,128)(2,1)}), (bf16[2048,3,256]{2,0,1:T(8,128)(2,1)}, ...) | async-done | bytes 12845072 | tf_op jit(solution)/shard_map/psum | solution.py:289
  1225.0 2.9 convert_element_type.164
  1228.0 3.7 convert_element_type.161
  1231.7 3.3 convert_element_type.168
  1235.0 6.0 convert_element_type.166
  (232 shorter events, 74.7 us)
Async XLA Ops:
  7.2 332.3 %copy-start = (bf16[704,2048]{1,0:T(8,128)(2,1)S(1)}, bf16[704,2048]{1,0:T(8,128)(2,1)}, u32[]{:S(2)}) copy-start(bf16[704,2048]{1,0:T(8,128)(2,1)} %param.22) | copy-start | bytes 8650756
  7.2 1.6 copy-start.38
  7.2 2.3 copy-start.36
  7.2 12.8 %copy-start.5 = (bf16[128,2048]{1,0:T(8,128)(2,1)S(1)}, bf16[128,2048]{1,0:T(8,128)(2,1)}, u32[]{:S(2)}) copy-start(bf16[128,2048]{1,0:T(8,128)(2,1)} %param.15) | copy-start | bytes 1572868
  7.2 14.6 %copy-start.30 = (f32[2,2048]{1,0:T(2,128)S(1)}, f32[2,2048]{1,0:T(2,128)}, u32[]{:S(2)}) copy-start(f32[2,2048]{1,0:T(2,128)} %param.16) | copy-start | bytes 49156
  7.2 14.6 %copy-start.31 = (f32[2,2048]{1,0:T(2,128)S(1)}, f32[2,2048]{1,0:T(2,128)}, u32[]{:S(2)}) copy-start(f32[2,2048]{1,0:T(2,128)} %param.17) | copy-start | bytes 49156
  7.3 135.7 %all-gather.5.cloned.1.call-start = ((), (), s32[]{:S(2)}) async-start(), calls=%async_computation.9 | async-start | bytes 28311552 | tf_op jit(solution)/shard_map/all_gather | solution.py:186
  8.0 239.8 %all-gather.7.cloned.1.call-start = ((), (), s32[]{:S(2)}) async-start(), calls=%async_computation.10 | async-start | bytes 9437184 | tf_op jit(solution)/shard_map/all_gather | solution.py:188
  20.2 136.2 %copy-start.32 = (f32[128]{0:T(128)}, f32[128]{0:T(128)S(1)}, u32[]{:S(2)}) copy-start(f32[128]{0:T(128)S(1)} %broadcast_multiply_fusion.6) | copy-start | bytes 1540
  20.5 135.9 %copy-start.34 = (f32[128]{0:T(128)}, f32[128]{0:T(128)S(1)}, u32[]{:S(2)}) copy-start(f32[128]{0:T(128)S(1)} %add_rsqrt_fusion.1) | copy-start | bytes 1540
  21.9 141.2 %copy-start.25 = (f32[128,8]{0,1:T(8,128)}, f32[128,8]{0,1:T(8,128)S(1)}, u32[]{:S(2)}) copy-start(f32[128,8]{0,1:T(8,128)S(1)} %get-tuple-element.253) | copy-start | bytes 12292
  21.9 134.5 %copy-start.21 = (f32[1,2048]{1,0:T(1,128)}, f32[1,2048]{1,0:T(1,128)S(1)}, u32[]{:S(2)}) copy-start(f32[1,2048]{1,0:T(1,128)S(1)} %get-tuple-element.244) | copy-start | bytes 24580
  21.9 134.4 %copy-start.23 = (f32[1,2048]{1,0:T(1,128)}, f32[1,2048]{1,0:T(1,128)S(1)}, u32[]{:S(2)}) copy-start(f32[1,2048]{1,0:T(1,128)S(1)} %get-tuple-element.246) | copy-start | bytes 24580
  164.7 40.2 %all-to-all-start = ((bf16[128,3,8,256]{0,3,1,2:T(8,128)(2,1)}), bf16[128,3,8,256]{0,3,1,2:T(8,128)(2,1)}, u32[]{:S(2)}, u32[]{:S(2)}) async-start(bf16[128,3,8,256]{0,3,1,2:T(8,128)(2,1)} %copy.91), calls=%async_computation | async-start | bytes 3145728 | tf_op jit(solution)/shard_map/all_to_all | solution.py:202
  220.1 2.4 copy-start.7
  220.1 2.4 copy-start.16
  230.9 2.4 copy-start.7
  230.9 2.4 copy-start.16
  243.5 13.9 %all-to-all-start.1 = ((bf16[8,128,256]{1,2,0:T(8,128)(2,1)}), bf16[8,128,256]{1,2,0:T(8,128)(2,1)}, u32[]{:S(2)}, u32[]{:S(2)}) async-start(bf16[8,128,256]{1,2,0:T(8,128)(2,1)} %copy.94), calls=%async_computation.1 | async-start | bytes 1048576 | tf_op jit(solution)/shard_map/all_to_all | solution.py:212
  247.7 52.7 %all-gather.9.cloned.1.call-start = ((), (), s32[]{:S(2)}) async-start(), calls=%async_computation.11 | async-start | bytes 4718592 | tf_op jit(solution)/shard_map/all_gather | solution.py:144
  264.4 75.0 %all-gather.11.cloned.1.call-start = ((), (), s32[]{:S(2)}) async-start(), calls=%async_computation.13 | async-start | bytes 4718592 | tf_op jit(solution)/shard_map/all_gather | solution.py:144
  266.5 145.4 %reduce-scatter.10.cloned.1.call-start = ((), (), s32[]{:S(2)}) async-start(), calls=%async_computation.14 | async-start | bytes 4718592 | tf_op jit(solution)/shard_map/reduce_scatter | solution.py:148
  347.8 1.6 copy-start.40
  360.4 107.0 %reduce-scatter.8.cloned.1.call-start = ((), (), s32[]{:S(2)}) async-start(), calls=%async_computation.12 | async-start | bytes 4718592 | tf_op jit(solution)/shard_map/reduce_scatter | solution.py:148
  366.8 45.0 %copy-start.4 = (f32[128,2048]{1,0:T(8,128)S(1)}, f32[128,2048]{1,0:T(8,128)}, u32[]{:S(2)}) copy-start(f32[128,2048]{1,0:T(8,128)} %copy-done.3) | copy-start | bytes 3145732
  366.8 100.5 %copy-start.18 = (bf16[128,2048]{1,0:T(8,128)(2,1)S(1)}, bf16[128,2048]{1,0:T(8,128)(2,1)}, u32[]{:S(2)}) copy-start(bf16[128,2048]{1,0:T(8,128)(2,1)} %param.25) | copy-start | bytes 1572868
  366.9 245.1 %reduce-scatter.14.cloned.1.call-start = ((), (), s32[]{:S(2)}) async-start(), calls=%async_computation.16 | async-start | bytes 9437184 | tf_op jit(solution)/shard_map/reduce_scatter | solution.py:282
  469.7 7.2 copy-start.9
  483.1 18.0 %copy-start.2 = (bf16[1024,4,64]{0,2,1:T(8,128)(2,1)S(1)}, bf16[1024,4,64]{0,2,1:T(8,128)(2,1)}, u32[]{:S(2)}) copy-start(bf16[1024,4,64]{0,2,1:T(8,128)(2,1)} %get-tuple-element.490) | copy-start | bytes 1572868
  483.1 18.0 %copy-start.8 = (bf16[1024,4,64]{0,2,1:T(8,128)(2,1)S(1)}, bf16[1024,4,64]{0,2,1:T(8,128)(2,1)}, u32[]{:S(2)}) copy-start(bf16[1024,4,64]{0,2,1:T(8,128)(2,1)} %get-tuple-element.491) | copy-start | bytes 1572868
  484.0 13.2 %all-to-all-start.2 = ((bf16[128,8,256]{2,0,1:T(8,128)(2,1)}), bf16[128,8,256]{2,0,1:T(8,128)(2,1)S(1)}, u32[]{:S(2)}, u32[]{:S(2)}) async-start(bf16[128,8,256]{2,0,1:T(8,128)(2,1)} %bitcast.142), calls=%async_computation.4 | async-start | bytes 1048576 | tf_op jit(solution)/shard_map/all_to_all | solution.py:255
  487.5 259.2 %reduce-scatter.12.cloned.1.call-start = ((), (), s32[]{:S(2)}) async-start(), calls=%async_computation.15 | async-start | bytes 28311552 | tf_op jit(solution)/shard_map/reduce_scatter | solution.py:276
  508.9 3.2 copy-start.20
  512.1 2.4 copy-start.14
  524.7 3.2 copy-start.20
  527.9 2.4 copy-start.14
  575.4 2.1 copy-start.26
  575.4 2.1 copy-start.29
  590.5 213.5 %reduce-scatter.16.cloned.1.call-start = ((), (), s32[]{:S(2)}) async-start(), calls=%async_computation.17 | async-start | bytes 589824
  602.8 622.3 %all-reduce.4.cloned.1.call-start = ((), (), s32[]{:S(2)}) async-start(), calls=%async_computation.18 | async-start | bytes 25690112 | tf_op jit(solution)/shard_map/psum | solution.py:289
  746.7 14.7 %copy-start.28 = (f32[2048]{0:T(1024)S(1)}, f32[2048]{0:T(1024)}, u32[]{:S(2)}) copy-start(f32[2048]{0:T(1024)} %get-tuple-element.165) | copy-start | bytes 24580
  746.7 14.7 %copy-start.27 = (f32[2048]{0:T(1024)S(1)}, f32[2048]{0:T(1024)}, u32[]{:S(2)}) copy-start(f32[2048]{0:T(1024)} %get-tuple-element.170) | copy-start | bytes 24580
  746.7 54.9 %copy-start.10 = (f32[128,2048]{1,0:T(8,128)S(1)}, f32[128,2048]{1,0:T(8,128)}, u32[]{:S(2)}) copy-start(f32[128,2048]{1,0:T(8,128)} %copy-done.9) | copy-start | bytes 3145732
  1225.0 2.9 copy-start.12
  1225.0 10.0 slice-start
  1228.0 3.7 copy-start.13
  1228.0 7.1 slice-start.1
  1235.0 6.0 copy-start.1
  (16 other events, 17.8 us)
Sparse Core Ops, SparseCore 0:
  10.0 132.9 all-gather.4
  144.9 68.7 all-gather.6
  264.5 35.7 all-gather.8
  302.7 36.7 all-gather.10
  360.5 51.3 reduce-scatter.9
  416.0 51.2 reduce-scatter.7
  476.9 71.4 reduce-scatter.13
  590.6 155.9 reduce-scatter.11
  750.0 34.2 reduce-scatter.15
  788.2 436.8 all-reduce.3
where the time goes:
time: 1250 us
  waiting for transfers between devices  879 us (70%)
  matrix products  145 us (12%)
  blocking collectives  92.4 us (7%)
  local copies, waits for them, and re-layouts  49.7 us (4%)
  other arithmetic  47.1 us (4%)
  between operations  15.2 us (1%)
  starting transfers between devices  13.4 us (1%)
    psum x1, waiting for transfers between devices, on_device(): lax.psum(mix_shard.astype(jnp.bfloat16), 'grp').astype(jnp.float32)  407 us
    reduce_scatter x1, waiting for transfers between devices, on_device(): lax.psum_scatter(mix_term.astype(jnp.bfloat16), 'seq', scatter_dimension=...  135 us
    all_gather x1, waiting for transfers between devices, on_device(): lax.all_gather(mix_weight, 'seq', axis=2, tiled=True)  121 us
    reduce_scatter x2, waiting for transfers between devices, summed_rows(): lax.psum_scatter(product(left).astype(jnp.bfloat16), 'seq', scatter_dimen...  98.3 us
    all_gather x2, waiting for transfers between devices, gather_rows(): return lax.all_gather(values, 'seq', axis=0, tiled=True)  61.5 us
    psum x1, blocking collectives, on_device(): lax.psum((jnp.stack([gain_one, gain_two]), jnp.stack([bias_one, bias_two]...  40.2 us
    all_to_all x1, waiting for transfers between devices, on_device(): lax.all_to_all(sending.reshape(slots_dev, 3, seq_count, local_width), 'se...  35.6 us
    all_to_all x1, blocking collectives, on_device(): lax.all_to_all(lowered, 'seq', split_axis=0, concat_axis=2, tiled=True)  29.5 us
  transfers between devices with their start and end apart: 13, of which 10 were waited for; matrix products, arithmetic and copies ran while one was open for 15% of the time, Pallas kernels for 0%

commit v1 on v0

--- a/solution.py
+++ b/solution.py
@@ -3,6 +3,7 @@
 import jax.numpy as jnp
 from jax import lax
 from jax.sharding import PartitionSpec as P
+from jax.lax import all_gather
 
 HEAD_DIM = 64
 ROT = 16
@@ -285,8 +286,13 @@
     )
     tokens_part, gain_one, bias_one = norm_back(normed_back, unit_one, scale_one, norm_gains[0])
     tokens_grad = (resid_back + tokens_part).astype(jnp.bfloat16)
+
+    def compute_chains(point):
+        piece_next = all_gather(point, "grp").sum(axis=0)
+        return piece_next
+
     mix_grad, mix_bias_grad, out_grad, gate_up_grad, down_grad = (
-        lax.psum(mix_shard.astype(jnp.bfloat16), "grp").astype(jnp.float32),
+        compute_chains(mix_shard.astype(jnp.bfloat16)).astype(jnp.float32),
         lax.psum(bias_shard.astype(jnp.bfloat16), "grp").astype(jnp.float32),
         lax.psum(out_shard.astype(jnp.bfloat16), "grp").astype(jnp.float32),
         lax.psum(gate_up_shard.astype(jnp.bfloat16), "grp").astype(jnp.float32),

time: 1250 us -> 1370 us (1.096)
  waiting for transfers between devices: 879 us -> 984 us
    all_gather x0 -> x1, waiting for transfers between devices: none -> 205 us  [compute_chains(): piece_next = all_gather(point, 'grp').sum(axis=0)]
    psum x1, waiting for transfers between devices: 407 us -> 306 us  [on_device(): lax.psum(out_shard.astype(jnp.bfloat16), 'grp').astype(jnp.float32)]
  transfers between devices with their start and end apart: 13 -> 14, of which waited for: 10 -> 11; matrix products, arithmetic and copies ran while one was open for 15% -> 15% of each run, Pallas kernels for 0% -> 0%
where the time goes in v1:
time: 1370 us; the launch traced here: 1360 us
  waiting for transfers between devices  984 us (72%)
  matrix products  145 us (11%)
  blocking collectives  91.7 us (7%)
  other arithmetic  58.7 us (4%)
  local copies, waits for them, and re-layouts  49.4 us (4%)
  between operations  14.9 us (1%)
    psum x1, waiting for transfers between devices, on_device(): lax.psum(out_shard.astype(jnp.bfloat16), 'grp').astype(jnp.float32)  306 us
    all_gather x1, waiting for transfers between devices, compute_chains(): piece_next = all_gather(point, 'grp').sum(axis=0)  205 us
    reduce_scatter x1, waiting for transfers between devices, on_device(): lax.psum_scatter(mix_term.astype(jnp.bfloat16), 'seq', scatter_dimension=...  135 us
    all_gather x1, waiting for transfers between devices, on_device(): lax.all_gather(mix_weight, 'seq', axis=2, tiled=True)  121 us
    reduce_scatter x2, waiting for transfers between devices, summed_rows(): lax.psum_scatter(product(left).astype(jnp.bfloat16), 'seq', scatter_dimen...  98.3 us
    all_gather x2, waiting for transfers between devices, gather_rows(): return lax.all_gather(values, 'seq', axis=0, tiled=True)  61.5 us
    psum x1, blocking collectives, on_device(): lax.psum((jnp.stack([gain_one, gain_two]), jnp.stack([bias_one, bias_two]...  40.2 us
    all_to_all x1, waiting for transfers between devices, on_device(): lax.all_to_all(sending.reshape(slots_dev, 3, seq_count, local_width), 'se...  35.6 us
  transfers between devices with their start and end apart: 14, of which 11 were waited for; matrix products, arithmetic and copies ran while one was open for 15% of the time, Pallas kernels for 0%

profile of v1, /device:TPU:0, one launch (start us, length us, event | category | flops | bytes accessed | tf_op | source)
XLA Modules:
  0.0 1362.7 jit_solution(18211757739679225277)
XLA Ops:
  9.5 10.4 all_gather.22
  21.9 121.0 %all-gather.7.cloned.1.call-done = bf16[2048,3,2048]{2,0,1:T(8,128)(2,1)} async-done(((bf16[2048,3,256]{2,0,1:T(8,128)(2,1)}), bf16[2048,3,2048]{2,0,1:T(8,128)(2,1)}) %all-gather.7.cloned.1.call-update) | async-done | bytes 25165840 | tf_op jit(solution)/shard_map/all_gather | solution.py:187
  143.0 13.4 convolution_add_fusion
  156.4 3.5 copy.90
  164.7 4.5 all-to-all-start
  169.3 35.6 %all-to-all-done = bf16[128,3,8,256]{0,3,1,2:T(8,128)(2,1)} async-done(((bf16[128,3,8,256]{0,3,1,2:T(8,128)(2,1)}), bf16[128,3,8,256]{0,3,1,2:T(8,128)(2,1)}, u32[]{:S(2)}, u32[]{:S(2)}) %all-to-all-start) | async-done | bytes 1572896 | tf_op jit(solution)/shard_map/all_to_all | solution.py:203
  204.9 3.6 copy.92
  208.5 3.7 reshape.381
  212.2 2.6 slice_bitcast_fusion.6
  215.6 21.5 %while.27 = (s32[]{:T(128)}, bf16[2,512,4,64]{1,3,2,0:T(8,128)(2,1)}, f32[2,4,512]{2,1,0:T(4,128)S(1)}, s32[2]{0:T(128)S(1)}, s32[1024]{0:T(1024)S(1)}, /*index=...) while((s32[]{:T(128)}, ...), condition=%wide.region_10.11_spmd, body=%wide.region_7.10_spmd.sunk | while | flops 563608064 | bytes 35469596 | solution.py:90
  217.5 2.6 fusion.126
  222.5 3.0 fusion.128
  228.2 2.6 fusion.126
  233.3 3.0 fusion.128
  243.5 4.1 all-to-all-start.1
  247.8 9.7 all-to-all-done.1
  257.4 4.9 fusion.81
  266.9 33.4 %all-gather.11.cloned.1.call-done = bf16[1024,2048]{1,0:T(8,128)(2,1)} async-done(((bf16[128,2048]{1,0:T(8,128)(2,1)}), bf16[1024,2048]{1,0:T(8,128)(2,1)}) %all-gather.11.cloned.1.call-update) | async-done | bytes 4194320 | tf_op jit(solution)/shard_map/all_gather | solution.py:145
  300.4 11.0 fusion.39
  311.4 28.1 %all-gather.13.cloned.1.call-done = bf16[1024,2048]{1,0:T(8,128)(2,1)} async-done(((bf16[128,2048]{1,0:T(8,128)(2,1)}), bf16[1024,2048]{1,0:T(8,128)(2,1)}) %all-gather.13.cloned.1.call-update) | async-done | bytes 4194320 | tf_op jit(solution)/shard_map/all_gather | solution.py:145
  339.4 8.3 fusion.45
  349.4 11.0 bitcast_convert_fusion
  360.4 6.4 convolution_convert_fusion.3
  366.9 45.0 %reduce-scatter.10.cloned.1.call-done = bf16[128,2048]{1,0:T(8,128)(2,1)} async-done(((bf16[1024,2048]{1,0:T(8,128)(2,1)}), bf16[128,2048]{1,0:T(8,128)(2,1)}) %reduce-scatter.10.cloned.1.call-update) | async-done | bytes 524304 | tf_op jit(solution)/shard_map/reduce_scatter | solution.py:149
  414.0 53.4 %reduce-scatter.8.cloned.1.call-done = bf16[128,2048]{1,0:T(8,128)(2,1)} async-done(((bf16[1024,2048]{1,0:T(8,128)(2,1)}), bf16[128,2048]{1,0:T(8,128)(2,1)}) %reduce-scatter.8.cloned.1.call-update) | async-done | bytes 524304 | tf_op jit(solution)/shard_map/reduce_scatter | solution.py:149
  469.7 7.1 convolution_convert_fusion.1
  476.8 6.3 convolution_convert_fusion.5
  483.9 3.5 all-to-all-start.2
  487.7 9.4 all-to-all-done.2
  501.1 31.0 %while.28 = (s32[]{:T(128)}, f32[1024,4,64]{0,2,1:T(8,128)S(1)}, f32[1024,4,64]{0,2,1:T(8,128)}, bf16[2,512,4,64]{1,3,2,0:T(8,128)(2,1)}, s32[2]{0:T(128)S(1)}, ...) while((s32[]{:T(128)}, f32[1024,4,64]{0,2,1:T(8,128)S(1)}, ...), condition=%wide.region_19.20_spmd.clone, body=%wide.region_17.19_spmd.clone.sunk | while | flops 1376647680 | bytes 87103920 | solution.py:125
  508.6 3.2 multiply_reduce_fusion.4
  524.1 3.2 multiply_reduce_fusion.4
  536.8 2.9 copy.98
  539.7 30.3 %all_to_all.56 = bf16[1024,3,1,256]{3,1,2,0:T(4,128)(2,1)S(1)} all-to-all(bf16[1024,3,1,256]{3,1,2,0:T(4,128)(2,1)S(1)} %copy.98), channel_id=1, replica_groups=mesh['grp'=4,'seq'=8] {'seq'}, dimensions={0} | all-to-all | bytes 3145728 | tf_op jit(solution)/shard_map/all_to_all | solution.py:267
  578.4 11.9 convolution_convert_fusion
  590.4 10.8 convolution_convert_fusion.2
  602.6 8.9 convolution_convert_fusion.4
  611.8 134.6 %reduce-scatter.12.cloned.1.call-done = bf16[2048,3,256]{2,0,1:T(8,128)(2,1)} async-done(((bf16[2048,3,2048]{2,0,1:T(8,128)(2,1)}), bf16[2048,3,256]{2,0,1:T(8,128)(2,1)}) %reduce-scatter.12.cloned.1.call-update) | async-done | bytes 3145744 | tf_op jit(solution)/shard_map/reduce_scatter | solution.py:277
  746.5 14.6 %fusion.59 = (f32[2048]{0:T(1024)S(1)}, f32[128]{0:T(128)S(1)}, f32[128]{0:T(128)S(1)}, f32[2048]{0:T(1024)S(1)}, f32[128,2048]{1,0:T(8,128)}) fusion(bf16[128,2048]{1,0:T(8,128)(2,1)S(1)} %copy-done.6, f32[128]{0:T(128)S(1)} %copy-done.34, f32[128]{0:T(128)S(1)} %copy-done.32, f32[2048]{0:T(1024)S(1)} %bitcast.195, ...), kind=kOutput, calls=%fused_computation.93 | convolution fusion | flops 3225415680 | bytes 28338176 | tf_op jit(solution)/shard_map/tcf,dcf->td/dot_general | solution.py:273
  761.2 40.2 %all-reduce = (f32[2,2048]{1,0:T(2,128)}, f32[2,2048]{1,0:T(2,128)}) all-reduce(f32[2,2048]{1,0:T(2,128)S(1)} %pad_maximum_fusion.10, f32[2,2048]{1,0:T(2,128)S(1)} %pad_maximum_fusion.11), channel_id=1, replica_groups=mesh['grp'=4,'seq'=8] {'grp','seq'}, use_global_device_ids=true, to_apply=%region_24.25 | all-reduce | flops 8192 | bytes 65536 | tf_op jit(solution)/shard_map/psum | solution.py:301
  804.8 10.9 psum.44
  816.3 306.4 %all-reduce.4.cloned.1.call-done = (bf16[256,2048]{1,0:T(8,128)(2,1)}, bf16[2048,2,704]{0,2,1:T(8,128)(2,1)}, bf16[704,2048]{1,0:T(8,128)(2,1)}) async-done(((bf16[256,2048]{1,0:T(8,128)(2,1)}, bf16[2048,2,704]{0,2,1:T(8,128)(2,1)}, bf16[704,2048]{1,0:T(8,128)(2,1)}), (bf16[256,2048]{1,0:T(8,128)(2,1)}, bf16[2048,2,704]{0,2,1:T(8,128)(2,1)}, bf16[704,2048]{1,0:T(8,128)(2,1)})) %all-reduce.4.cloned.1.call-update) | async-done | bytes 9699344 | tf_op jit(solution)/shard_map/psum | solution.py:297
  1122.7 2.9 convert_element_type.166
  1125.6 3.3 convert_element_type.170
  1128.9 7.0 convert_element_type.168
  1136.0 205.5 %all-gather.15.cloned.1.call-done = bf16[8192,3,256]{2,0,1:T(8,128)(2,1)} async-done(((bf16[2048,3,256]{2,0,1:T(8,128)(2,1)}), bf16[8192,3,256]{2,0,1:T(8,128)(2,1)}) %all-gather.15.cloned.1.call-update) | async-done | bytes 12582928 | tf_op jit(solution)/shard_map/all_gather | solution.py:291
  1341.4 9.1 reduce_sum.216
  1350.6 5.1 convert_element_type.163
  (234 shorter events, 79.5 us)
Async XLA Ops:
  7.2 332.3 %copy-start = (bf16[704,2048]{1,0:T(8,128)(2,1)S(1)}, bf16[704,2048]{1,0:T(8,128)(2,1)}, u32[]{:S(2)}) copy-start(bf16[704,2048]{1,0:T(8,128)(2,1)} %param.22) | copy-start | bytes 8650756
  7.2 1.6 copy-start.37
  7.2 2.3 copy-start.35
  7.2 12.8 copy-start.5
  7.2 14.6 %copy-start.29 = (f32[2,2048]{1,0:T(2,128)S(1)}, f32[2,2048]{1,0:T(2,128)}, u32[]{:S(2)}) copy-start(f32[2,2048]{1,0:T(2,128)} %param.16) | copy-start | bytes 49156
  7.2 14.6 %copy-start.30 = (f32[2,2048]{1,0:T(2,128)S(1)}, f32[2,2048]{1,0:T(2,128)}, u32[]{:S(2)}) copy-start(f32[2,2048]{1,0:T(2,128)} %param.17) | copy-start | bytes 49156
  7.3 135.7 %all-gather.7.cloned.1.call-start = ((), (), s32[]{:S(2)}) async-start(), calls=%async_computation.9 | async-start | bytes 28311552 | tf_op jit(solution)/shard_map/all_gather | solution.py:187
  8.0 239.8 %all-gather.9.cloned.1.call-start = ((), (), s32[]{:S(2)}) async-start(), calls=%async_computation.10 | async-start | bytes 9437184 | tf_op jit(solution)/shard_map/all_gather | solution.py:189
  20.2 136.2 %copy-start.31 = (f32[128]{0:T(128)}, f32[128]{0:T(128)S(1)}, u32[]{:S(2)}) copy-start(f32[128]{0:T(128)S(1)} %broadcast_multiply_fusion.6) | copy-start | bytes 1540
  20.5 135.9 %copy-start.33 = (f32[128]{0:T(128)}, f32[128]{0:T(128)S(1)}, u32[]{:S(2)}) copy-start(f32[128]{0:T(128)S(1)} %add_rsqrt_fusion.1) | copy-start | bytes 1540
  21.9 141.2 %copy-start.24 = (f32[128,8]{0,1:T(8,128)}, f32[128,8]{0,1:T(8,128)S(1)}, u32[]{:S(2)}) copy-start(f32[128,8]{0,1:T(8,128)S(1)} %get-tuple-element.252) | copy-start | bytes 12292
  21.9 134.5 %copy-start.20 = (f32[1,2048]{1,0:T(1,128)}, f32[1,2048]{1,0:T(1,128)S(1)}, u32[]{:S(2)}) copy-start(f32[1,2048]{1,0:T(1,128)S(1)} %get-tuple-element.243) | copy-start | bytes 24580
  21.9 134.4 %copy-start.22 = (f32[1,2048]{1,0:T(1,128)}, f32[1,2048]{1,0:T(1,128)S(1)}, u32[]{:S(2)}) copy-start(f32[1,2048]{1,0:T(1,128)S(1)} %get-tuple-element.245) | copy-start | bytes 24580
  164.7 40.2 %all-to-all-start = ((bf16[128,3,8,256]{0,3,1,2:T(8,128)(2,1)}), bf16[128,3,8,256]{0,3,1,2:T(8,128)(2,1)}, u32[]{:S(2)}, u32[]{:S(2)}) async-start(bf16[128,3,8,256]{0,3,1,2:T(8,128)(2,1)} %copy.91), calls=%async_computation | async-start | bytes 3145728 | tf_op jit(solution)/shard_map/all_to_all | solution.py:203
  220.1 2.4 copy-start.7
  220.1 2.4 copy-start.15
  230.9 2.4 copy-start.7
  230.9 2.4 copy-start.15
  243.5 13.9 %all-to-all-start.1 = ((bf16[8,128,256]{1,2,0:T(8,128)(2,1)}), bf16[8,128,256]{1,2,0:T(8,128)(2,1)}, u32[]{:S(2)}, u32[]{:S(2)}) async-start(bf16[8,128,256]{1,2,0:T(8,128)(2,1)} %copy.94), calls=%async_computation.1 | async-start | bytes 1048576 | tf_op jit(solution)/shard_map/all_to_all | solution.py:213
  247.7 52.7 %all-gather.11.cloned.1.call-start = ((), (), s32[]{:S(2)}) async-start(), calls=%async_computation.11 | async-start | bytes 4718592 | tf_op jit(solution)/shard_map/all_gather | solution.py:145
  264.4 75.0 %all-gather.13.cloned.1.call-start = ((), (), s32[]{:S(2)}) async-start(), calls=%async_computation.13 | async-start | bytes 4718592 | tf_op jit(solution)/shard_map/all_gather | solution.py:145
  266.5 145.4 %reduce-scatter.10.cloned.1.call-start = ((), (), s32[]{:S(2)}) async-start(), calls=%async_computation.14 | async-start | bytes 4718592 | tf_op jit(solution)/shard_map/reduce_scatter | solution.py:149
  347.8 1.6 copy-start.39
  360.4 107.0 %reduce-scatter.8.cloned.1.call-start = ((), (), s32[]{:S(2)}) async-start(), calls=%async_computation.12 | async-start | bytes 4718592 | tf_op jit(solution)/shard_map/reduce_scatter | solution.py:149
  366.8 45.0 %copy-start.4 = (f32[128,2048]{1,0:T(8,128)S(1)}, f32[128,2048]{1,0:T(8,128)}, u32[]{:S(2)}) copy-start(f32[128,2048]{1,0:T(8,128)} %copy-done.3) | copy-start | bytes 3145732
  366.8 100.5 %copy-start.17 = (bf16[128,2048]{1,0:T(8,128)(2,1)S(1)}, bf16[128,2048]{1,0:T(8,128)(2,1)}, u32[]{:S(2)}) copy-start(bf16[128,2048]{1,0:T(8,128)(2,1)} %param.25) | copy-start | bytes 1572868
  366.8 244.7 %reduce-scatter.14.cloned.1.call-start = ((), (), s32[]{:S(2)}) async-start(), calls=%async_computation.16 | async-start | bytes 9437184 | tf_op jit(solution)/shard_map/reduce_scatter | solution.py:283
  469.7 7.2 copy-start.9
  483.1 18.0 %copy-start.2 = (bf16[1024,4,64]{0,2,1:T(8,128)(2,1)S(1)}, bf16[1024,4,64]{0,2,1:T(8,128)(2,1)}, u32[]{:S(2)}) copy-start(bf16[1024,4,64]{0,2,1:T(8,128)(2,1)} %get-tuple-element.488) | copy-start | bytes 1572868
  483.1 18.0 %copy-start.8 = (bf16[1024,4,64]{0,2,1:T(8,128)(2,1)S(1)}, bf16[1024,4,64]{0,2,1:T(8,128)(2,1)}, u32[]{:S(2)}) copy-start(bf16[1024,4,64]{0,2,1:T(8,128)(2,1)} %get-tuple-element.489) | copy-start | bytes 1572868
  483.9 13.2 all-to-all-start.2
  487.4 259.0 %reduce-scatter.12.cloned.1.call-start = ((), (), s32[]{:S(2)}) async-start(), calls=%async_computation.15 | async-start | bytes 28311552 | tf_op jit(solution)/shard_map/reduce_scatter | solution.py:277
  508.6 3.2 copy-start.19
  511.8 2.4 copy-start.13
  524.1 3.2 copy-start.19
  527.3 2.4 copy-start.13
  575.4 2.1 copy-start.25
  575.4 2.1 copy-start.28
  590.3 213.5 %reduce-scatter.16.cloned.1.call-start = ((), (), s32[]{:S(2)}) async-start(), calls=%async_computation.18 | async-start | bytes 589824
  602.6 520.1 %all-reduce.4.cloned.1.call-start = ((), (), s32[]{:S(2)}) async-start(), calls=%async_computation.19 | async-start | bytes 19398656 | tf_op jit(solution)/shard_map/psum | solution.py:297
  611.5 729.9 %all-gather.15.cloned.1.call-start = ((), (), s32[]{:S(2)}) async-start(), calls=%async_computation.17 | async-start | bytes 15728640 | tf_op jit(solution)/shard_map/all_gather | solution.py:291
  746.5 14.7 %copy-start.27 = (f32[2048]{0:T(1024)S(1)}, f32[2048]{0:T(1024)}, u32[]{:S(2)}) copy-start(f32[2048]{0:T(1024)} %get-tuple-element.165) | copy-start | bytes 24580
  746.5 14.7 %copy-start.26 = (f32[2048]{0:T(1024)S(1)}, f32[2048]{0:T(1024)}, u32[]{:S(2)}) copy-start(f32[2048]{0:T(1024)} %get-tuple-element.170) | copy-start | bytes 24580
  746.5 54.9 %copy-start.10 = (f32[128,2048]{1,0:T(8,128)S(1)}, f32[128,2048]{1,0:T(8,128)}, u32[]{:S(2)}) copy-start(f32[128,2048]{1,0:T(8,128)} %copy-done.9) | copy-start | bytes 3145732
  1122.7 2.9 copy-start.12
  1122.7 6.3 slice-start
  1125.6 3.3 slice-start.1
  1341.4 14.3 %copy-start.1 = (bf16[704,2048]{1,0:T(8,128)(2,1)S(1)}, bf16[704,2048]{1,0:T(8,128)(2,1)}, u32[]{:S(2)}) copy-start(bf16[704,2048]{1,0:T(8,128)(2,1)} %param.22) | copy-start | bytes 8650756
  (16 other events, 17.8 us)
Sparse Core Ops, SparseCore 0:
  10.0 132.9 all-gather.6
  144.9 68.7 all-gather.8
  264.5 35.7 all-gather.10
  302.7 36.7 all-gather.12
  360.5 51.3 reduce-scatter.9
  416.0 51.2 reduce-scatter.7
  476.9 72.3 reduce-scatter.13
  590.5 155.9 reduce-scatter.11
  749.8 34.2 reduce-scatter.15
  788.0 334.6 all-reduce.3
  1124.3 217.1 all-gather.14
